TPU v7x, 32 devices: a whole 2x2x4 slice. The times are simulated.
32 devices in a mesh: dp: 8 (over z, y), tensor: 4 (over x, core).
Axes of the slice: x: 2, y: 2, z: 4, core: 2. Of those that a mesh axis runs over, the one named last changes fastest.
Arguments:
- tokens: bfloat16 [8, 4, 512, 768], P(None, 'tensor', 'dp'), may hold values from -6 to 6
- cotangent: bfloat16 [8, 2048, 768], P('dp', 'tensor'), may hold values from -6 to 6
- lengths: int32 [8], replicated, may hold values from 1 to 2048, 12288 in all
- dealt_to: int32 [8], replicated, may hold values from 0 to 7, each once
- adapter_id: int32 [8], replicated, may hold values from 0 to 7
- norm_gain: bfloat16 [768], replicated, may hold values from 0.25 to 1.75
- w_zx: bfloat16 [768, 2, 1536], P('dp', None, 'tensor'), may hold values from -0.21875 to 0.21875
- w_dt: bfloat16 [768, 24], P('dp', 'tensor'), may hold values from -0.21875 to 0.21875
- w_bc: bfloat16 [768, 256], P('dp'), may hold values from -0.21875 to 0.21875
- x_kernel: float32 [4, 1536], P(None, 'tensor'), may hold values from -3 to 3
- x_offset: float32 [1536], P('tensor'), may hold values from -0.5 to 0.5
- bc_kernel: float32 [4, 256], replicated, may hold values from -3 to 3
- bc_offset: float32 [256], replicated, may hold values from -0.5 to 0.5
- dt_bias: float32 [24], P('tensor'), may hold values from -6.9 to -2.3
- a_log: float32 [24], P('tensor'), may hold values from 0 to 2.77
- d_skip: float32 [24], P('tensor'), may hold values from 0.5 to 1.5
- out_gain: bfloat16 [1536], P('tensor'), may hold values from 0.25 to 1.75
- w_out: bfloat16 [1536, 768], P('tensor', 'dp'), may hold values from -0.15625 to 0.15625
- inlet_down: bfloat16 [8, 768, 16], replicated, may hold values from -0.21875 to 0.21875
- inlet_up: bfloat16 [8, 16, 2, 1536], P(None, None, None, 'tensor'), may hold values from -1.5 to 1.5
- outlet_down: bfloat16 [8, 1536, 16], replicated, may hold values from -0.15625 to 0.15625
- outlet_up: bfloat16 [8, 16, 768], replicated, may hold values from -1.5 to 1.5
Outputs:
- output: bfloat16 [8, 2048, 768], P('dp', 'tensor')
- token_grads: bfloat16 [8, 4, 512, 768], P(None, 'tensor', 'dp')
- inlet_dgrad: float32 [8, 768, 16], replicated
- inlet_ugrad: float32 [8, 16, 2, 1536], P(None, None, None, 'tensor')
- outlet_dgrad: float32 [8, 1536, 16], replicated
- outlet_ugrad: float32 [8, 16, 768], replicated
Inputs may be any that keep to these rules, and one draw needn't show every extreme that they name: `lengths`: the longest sequence has exactly 2048 positions. `dealt_to`: every group is named by exactly one sequence.
All inputs are finite; a program needn't handle non-finite values.
Results may differ from a plain program's by a relative error of at most 0.0085.
Values may be sent and summed in bfloat16 or wider, within the bound.
A program may use at most 128 MiB of HBM per device.

v0:
```python
from functools import partial
import jax
import jax.numpy as jnp
from jax import lax
from jax.sharding import PartitionSpec as P

INNER = 1536
SPAN = 256
ADAPTERS = 8
EPSILON = 1e-05
HIGHEST = lax.Precision.HIGHEST


def causal_conv(values, kernel, offsets):
    kernel_width = kernel.shape[0]
    length = values.shape[0]
    padded = jnp.pad(values, ((kernel_width - 1, 0), (0, 0)))
    running = jnp.zeros_like(values) + offsets[None, :]
    for offset in range(kernel_width):
        running = running + kernel[offset][None, :] * padded[offset : offset + length]
    return running


def state_mixer(heads_x, step_size, decay_rates, input_b, input_c):
    length, head_count, head_dim = heads_x.shape
    blocks = length // SPAN
    state_dim = input_b.shape[1]
    block_x = heads_x.reshape(blocks, SPAN, head_count, head_dim)
    block_dt = step_size.reshape(blocks, SPAN, head_count)
    block_b = input_b.reshape(blocks, SPAN, state_dim)
    block_c = input_c.reshape(blocks, SPAN, state_dim)
    causal = jnp.arange(SPAN)[:, None] >= jnp.arange(SPAN)[None, :]
    within = jnp.einsum(
        "ts,csh->cth",
        causal.astype(jnp.float32),
        block_dt * decay_rates[None, None, :],
        precision=HIGHEST,
    )
    scores = jnp.einsum("ctn,csn->cts", block_c, block_b, precision=HIGHEST)
    causal_full = causal[None, :, :, None]
    spread = within[:, :, None, :] - within[:, None, :, :]
    mixing = jnp.where(causal_full, jnp.exp(jnp.where(causal_full, spread, 0.0)), 0.0)
    weights = scores[:, :, :, None] * mixing * block_dt[:, None, :, :]
    inside = jnp.einsum("ctsh,cshp->cthp", weights, block_x, precision=HIGHEST)
    span_total = within[:, -1, :]
    tail_weight = jnp.exp(span_total[:, None, :] - within) * block_dt
    fresh_state = jnp.einsum("cth,cthp,ctn->chpn", tail_weight, block_x, block_b, precision=HIGHEST)
    span_ids = jnp.arange(blocks)
    through = jnp.einsum(
        "dc,ch->dh",
        (span_ids[:, None] >= span_ids[None, :]).astype(jnp.float32),
        span_total,
        precision=HIGHEST,
    )
    before = through - span_total
    earlier = (span_ids[:, None] > span_ids[None, :])[:, :, None]
    passing = jnp.where(
        earlier, jnp.exp(jnp.where(earlier, before[:, None, :] - through[None, :, :], 0.0)), 0.0
    )
    state_in = jnp.einsum("dch,chpn->dhpn", passing, fresh_state, precision=HIGHEST)
    carried = (
        jnp.einsum("ctn,chpn->cthp", block_c, state_in, precision=HIGHEST)
        * jnp.exp(within)[:, :, :, None]
    )
    return (inside + carried).reshape(length, head_count, head_dim)


def mixer_part(weights_local, p_zx, p_bc, p_dt):
    x_kernel, x_offset, bc_kernel, bc_offset, dt_bias, a_log, d_skip = weights_local
    length = p_zx.shape[0]
    inner_local = p_zx.shape[2]
    head_count = p_dt.shape[1]
    state_dim = p_bc.shape[1] // 2
    inner_x = jax.nn.silu(causal_conv(p_zx[:, 1, :], x_kernel, x_offset))
    mixed_bc = jax.nn.silu(causal_conv(p_bc, bc_kernel, bc_offset))
    step_size = jax.nn.softplus(p_dt + dt_bias)
    heads_x = inner_x.reshape(length, head_count, inner_local // head_count)
    mixed = state_mixer(
        heads_x, step_size, -jnp.exp(a_log), mixed_bc[:, :state_dim], mixed_bc[:, state_dim:]
    )
    mixed = mixed + d_skip[None, :, None] * heads_x
    return mixed.reshape(length, inner_local) * jax.nn.silu(p_zx[:, 0, :])


def shards(
    tokens,
    cotangent,
    lengths,
    dealt_to,
    adapter_id,
    norm_gain,
    w_zx,
    w_dt,
    w_bc,
    x_kernel,
    x_offset,
    bc_kernel,
    bc_offset,
    dt_bias,
    a_log,
    d_skip,
    out_gain,
    w_out,
    inlet_down,
    inlet_up,
    outlet_down,
    outlet_up,
):
    model_dim = tokens.shape[3]
    inner_local = w_zx.shape[2]
    full_zx, full_dt, full_bc, full_out = (
        lax.all_gather(w_zx, "dp", axis=0, tiled=True),
        lax.all_gather(w_dt, "dp", axis=0, tiled=True),
        lax.all_gather(w_bc, "dp", axis=0, tiled=True),
        lax.all_gather(w_out, "dp", axis=1, tiled=True),
    )
    seq_count = dealt_to.shape[0]
    slot_ids = jnp.arange(seq_count, dtype=jnp.int32)
    placed = (dealt_to[None, :] == slot_ids[:, None]).astype(jnp.int32)
    seq_of = jnp.sum(placed * slot_ids[None, :], axis=1)
    picked = jnp.take(tokens, seq_of, axis=0)
    arrived = lax.all_to_all(picked, "dp", split_axis=0, concat_axis=2, tiled=True)
    tok_rows = arrived.reshape(-1, model_dim)
    tok_dev = tok_rows.shape[0]
    group_id = lax.axis_index("dp")
    own_seq = jnp.take(seq_of, group_id)
    chosen = (jnp.arange(ADAPTERS, dtype=jnp.int32) == jnp.take(adapter_id, own_seq)).astype(
        jnp.float32
    )
    positions = lax.axis_index("tensor") * tok_dev + jnp.arange(tok_dev, dtype=jnp.int32)
    valid_rows = (positions < jnp.take(lengths, own_seq)).astype(jnp.float32)[:, None]

    def select_one(stacked):
        return jnp.einsum("k,k...->...", chosen, stacked.astype(jnp.float32)).astype(jnp.bfloat16)

    in_down = select_one(inlet_down)
    in_up = select_one(inlet_up)
    out_down = select_one(outlet_down)
    out_up = select_one(outlet_up)
    residual = tok_rows.astype(jnp.float32)
    gain_in = norm_gain.astype(jnp.float32)
    inv_in = lax.rsqrt(jnp.mean(residual * residual, axis=1, keepdims=True) + EPSILON)
    normed = (residual * inv_in * gain_in).astype(jnp.bfloat16)
    hidden_in = jnp.dot(normed, in_down, preferred_element_type=jnp.float32).astype(jnp.bfloat16)
    all_normed, all_hidden = (
        lax.all_gather(normed, "tensor", axis=0, tiled=True),
        lax.all_gather(hidden_in, "tensor", axis=0, tiled=True),
    )
    zx_matrix = full_zx.reshape(model_dim, 2 * inner_local)
    up_matrix = in_up.reshape(in_up.shape[0], 2 * inner_local)
    p_zx = jnp.dot(all_normed, zx_matrix, preferred_element_type=jnp.float32) + jnp.dot(
        all_hidden, up_matrix, preferred_element_type=jnp.float32
    )
    p_zx = p_zx.reshape(-1, 2, inner_local)
    p_bc = jnp.dot(all_normed, full_bc, preferred_element_type=jnp.float32)
    p_dt = jnp.dot(all_normed, full_dt, preferred_element_type=jnp.float32)
    mixer_weights = (x_kernel, x_offset, bc_kernel, bc_offset, dt_bias, a_log, d_skip)
    gated_act, mixer_pull = jax.vjp(partial(mixer_part, mixer_weights), p_zx, p_bc, p_dt)
    gain_rows = out_gain.astype(jnp.float32)
    squares = lax.psum(jnp.sum(gated_act * gated_act, axis=1), "tensor")
    inv_out = lax.rsqrt(squares / INNER + EPSILON)[:, None]
    normed_out = (gated_act * inv_out * gain_rows).astype(jnp.bfloat16)
    row_start = lax.axis_index("tensor") * inner_local
    down_rows = lax.dynamic_slice_in_dim(out_down, row_start, inner_local, 0)
    summed_out, summed_hidden = (
        lax.psum_scatter(
            jnp.dot(normed_out, full_out, preferred_element_type=jnp.float32),
            "tensor",
            scatter_dimension=0,
            tiled=True,
        ),
        lax.psum_scatter(
            jnp.dot(normed_out, down_rows, preferred_element_type=jnp.float32),
            "tensor",
            scatter_dimension=0,
            tiled=True,
        ),
    )
    hidden_out = summed_hidden.astype(jnp.bfloat16)
    branch_out = summed_out + jnp.dot(hidden_out, out_up, preferred_element_type=jnp.float32)
    output = (
        (residual + valid_rows * branch_out).astype(jnp.bfloat16).reshape(1, tok_dev, model_dim)
    )
    cot_rows = cotangent.reshape(tok_dev, model_dim).astype(jnp.float32)
    grad_branch = (cot_rows * valid_rows).astype(jnp.bfloat16)
    back_hidden = jnp.dot(grad_branch, out_up.T, preferred_element_type=jnp.float32).astype(
        jnp.bfloat16
    )
    outup_sum = jnp.dot(hidden_out.T, grad_branch, preferred_element_type=jnp.float32)
    wide_branch, wide_hidden = (
        lax.all_gather(grad_branch, "tensor", axis=0, tiled=True),
        lax.all_gather(back_hidden, "tensor", axis=0, tiled=True),
    )
    back_normed = jnp.dot(wide_branch, full_out.T, preferred_element_type=jnp.float32) + jnp.dot(
        wide_hidden, down_rows.T, preferred_element_type=jnp.float32
    )
    weighted_out = gain_rows * back_normed
    cross_sum = lax.psum(jnp.sum(weighted_out * gated_act, axis=1), "tensor")
    back_gated = inv_out * weighted_out - gated_act * inv_out**3 * (cross_sum / INNER)[:, None]
    local_rows = jnp.dot(normed_out.T, wide_hidden, preferred_element_type=jnp.float32)
    outdown_sum = lax.dynamic_update_slice_in_dim(
        jnp.zeros((INNER, local_rows.shape[1]), jnp.float32), local_rows, row_start, 0
    )
    grad_zx, grad_bc, grad_dt = mixer_pull(back_gated)
    low_zx3 = grad_zx.astype(jnp.bfloat16)
    low_zx = low_zx3.reshape(-1, 2 * inner_local)
    low_dt = grad_dt.astype(jnp.bfloat16)
    inup_sum = jnp.dot(all_hidden.T, low_zx, preferred_element_type=jnp.float32).reshape(
        -1, 2, inner_local
    )
    normed_part = jnp.dot(low_zx, zx_matrix.T, preferred_element_type=jnp.float32) + jnp.dot(
        low_dt, full_dt.T, preferred_element_type=jnp.float32
    )
    hidden_part = jnp.dot(low_zx, up_matrix.T, preferred_element_type=jnp.float32)
    grad_normed, grad_hidden, grad_bcrows = (
        lax.psum_scatter(normed_part, "tensor", scatter_dimension=0, tiled=True),
        lax.psum_scatter(hidden_part, "tensor", scatter_dimension=0, tiled=True),
        lax.psum_scatter(grad_bc, "tensor", scatter_dimension=0, tiled=True),
    )
    low_bc = grad_bcrows.astype(jnp.bfloat16)
    low_hidden = grad_hidden.astype(jnp.bfloat16)
    grad_normed = (
        grad_normed
        + jnp.dot(low_bc, full_bc.T, preferred_element_type=jnp.float32)
        + jnp.dot(low_hidden, in_down.T, preferred_element_type=jnp.float32)
    )
    indown_sum = jnp.dot(normed.T, low_hidden, preferred_element_type=jnp.float32)
    weighted = gain_in * grad_normed
    grad_input = (
        cot_rows
        + inv_in * weighted
        - residual * inv_in**3 * jnp.mean(weighted * residual, axis=1, keepdims=True)
    )
    sent_back = grad_input.astype(jnp.bfloat16).reshape(1, 1, tok_dev, model_dim)
    returned = lax.all_to_all(sent_back, "dp", split_axis=2, concat_axis=0, tiled=True)
    token_grads = jnp.take(returned, dealt_to, axis=0)
    inlet_dgrad, outlet_dgrad, outlet_ugrad = lax.psum(
        (
            chosen[:, None, None] * indown_sum[None],
            chosen[:, None, None] * outdown_sum[None],
            chosen[:, None, None] * outup_sum[None],
        ),
        ("dp", "tensor"),
    )
    inlet_ugrad = lax.psum(
        (chosen[:, None, None, None] * inup_sum[None]).astype(jnp.bfloat16), "dp"
    ).astype(jnp.float32)
    return (output, token_grads, inlet_dgrad, inlet_ugrad, outlet_dgrad, outlet_ugrad)


def solution(mesh):
    in_specs = (
        P(None, "tensor", "dp", None),
        P("dp", "tensor", None),
        P(),
        P(),
        P(),
        P(),
        P("dp", None, "tensor"),
        P("dp", "tensor"),
        P("dp", None),
        P(None, "tensor"),
        P("tensor"),
        P(),
        P(),
        P("tensor"),
        P("tensor"),
        P("tensor"),
        P("tensor"),
        P("tensor", "dp"),
        P(),
        P(None, None, None, "tensor"),
        P(),
        P(),
    )
    out_specs = (
        P("dp", "tensor", None),
        P(None, "tensor", "dp", None),
        P(),
        P(None, None, None, "tensor"),
        P(),
        P(),
    )
    return jax.shard_map(shards, mesh=mesh, in_specs=in_specs, out_specs=out_specs, check_vma=False)
```

profile of v0, /device:TPU:0, one launch (start us, length us, event | category | flops | bytes accessed | tf_op | source)
XLA Modules:
  0.0 787.3 jit_solution(1121650660833322522)
XLA Ops:
  17.4 7.4 all-to-all-start
  24.9 26.5 %all-to-all-done = bf16[8,1,64,768]{3,2,1,0:T(8,128)(2,1)S(1)} async-done(((bf16[8,1,64,768]{3,2,1,0:T(8,128)(2,1)}), bf16[8,1,64,768]{3,2,1,0:T(8,128)(2,1)S(1)}, u32[]{:S(2)}, u32[]{:S(2)}) %all-to-all-start) | async-done | bytes 786464 | tf_op jit(solution)/shard_map/all_to_all | solution.py:122
  56.1 26.0 %all-gather = bf16[8,96,6]{1,2,0:T(8,128)(2,1)S(1)} all-gather(bf16[1,96,6]{1,2,0:T(8,128)(2,1)S(1)} %bitcast.353), channel_id=1, replica_groups=mesh['dp'=8,'tensor'=4] {'dp'}, dimensions={0}, use_global_device_ids=true | all-gather | bytes 10368 | tf_op jit(solution)/shard_map/all_gather | solution.py:113
  85.3 5.8 all_gather.31
  93.0 31.3 %all_gather.27 = bf16[768,256]{1,0:T(8,128)(2,1)S(1)} all-gather(bf16[96,256]{1,0:T(8,128)(2,1)} %param.32), channel_id=1, replica_groups=mesh['dp'=8,'tensor'=4] {'dp'}, dimensions={0}, use_global_device_ids=true | all-gather | bytes 442368 | tf_op jit(solution)/shard_map/all_gather | solution.py:114
  126.0 31.6 %all_gather.29 = bf16[384,768]{0,1:T(8,128)(2,1)S(1)} all-gather(bf16[384,96]{0,1:T(8,128)(2,1)} %param.41), channel_id=1, replica_groups=mesh['dp'=8,'tensor'=4] {'dp'}, dimensions={1}, use_global_device_ids=true | all-gather | bytes 663552 | tf_op jit(solution)/shard_map/all_gather | solution.py:115
  158.0 5.9 all_gather.26
  166.2 5.4 fusion.223
  171.6 3.6 compare_select_fusion.2
  186.2 3.9 fusion.219
  191.2 3.0 fusion.215
  194.2 3.6 copy.268
  202.9 3.8 copy.269
  206.7 4.4 fusion.33
  211.1 4.0 copy.197
  215.1 3.5 copy.271
  220.5 3.8 fusion.41
  226.8 3.0 fusion.84
  229.9 15.3 %bitcast_add_fusion.2 = f32[8,256,6,64]{1,3,2,0:T(8,128)S(1)} fusion(f32[8,256,6,64]{1,3,2,0:T(8,128)S(1)} %fusion.84, f32[8,256,6]{1,2,0:T(8,128)S(1)} %bitcast.332, f32[8,256,6]{1,2,0:T(8,128)S(1)} %copy-done.64, f32[8,256,256]{2,1,0:T(8,128)S(1)} %fusion.221, pred[256,256]{1,0:T(8,128)(4,1)S(1)} %copy-done.65, f32[8,256,6,64]{1,0,3,2:T(8,128)S(1)} %bitcast.297, ...), kind=kOutput, calls=%fused_computation.50 | convolution fusion | flops 2433220608 | bytes 11747328 | tf_op jit(solution)/shard_map/jvp(ctsh,cshp->cthp)/dot_general | solution.py:44
  250.1 3.6 copy.213
  253.6 10.0 %multiply_reduce_fusion.3 = (f32[2048]{0:T(1024)}, f32[2048]{0:T(1024)}, f32[2048,384]{1,0:T(8,128)}, f32[2048,384]{1,0:T(8,128)}) fusion(f32[2048,1,384]{2,0,1:T(8,128)} %copy.269, f32[2048,384]{1,0:T(8,128)} %copy.213, f32[2048,384]{1,0:T(8,128)} %get-tuple-element.75, f32[384]{0:T(512)} %mul.552, f32[2048,384]{1,0:T(8,128)} %fusion.223, ...), kind=kOutput, calls=%fused_computation.55 | convolution fusion | flops 38531072 | bytes 19058692 | tf_op jit(solution)/shard_map/dot_general | solution.py:194
  263.6 13.0 %all-reduce.16 = (f32[2048]{0:T(1024)}, f32[2048]{0:T(1024)}) all-reduce(f32[2048]{0:T(1024)} %get-tuple-element.57, f32[2048]{0:T(1024)} %get-tuple-element.56), channel_id=1, replica_groups=mesh['dp'=8,'tensor'=4] {'tensor'}, use_global_device_ids=true, to_apply=%region_3.5 | all-reduce | flops 4096 | bytes 32768 | tf_op jit(solution)/shard_map/psum | solution.py:160
  277.3 9.0 %fusion.24 = (f32[2048,1,384]{2,0,1:T(8,128)}, f32[2048,384]{1,0:T(8,128)}, bf16[2048,384]{1,0:T(8,128)(2,1)}) fusion(f32[2048,1,384]{2,0,1:T(8,128)} %copy.269, f32[2048]{0:T(1024)S(1)} %get-tuple-element.106, f32[2048,384]{1,0:T(8,128)} %get-tuple-element.73, f32[2048]{0:T(1024)S(1)} %get-tuple-element.93, f32[2048,384]{1,0:T(8,128)} %get-tuple-element.103, ...), kind=kLoop, calls=%fused_computation.34 | loop fusion | flops 19660800 | bytes 23620608 | tf_op jit(solution)/shard_map/transpose(jvp())/broadcast_in_dim | solution.py:82
  286.3 4.0 copy.215
  290.3 3.4 copy.274
  293.8 7.0 fusion.88
  300.8 3.8 fusion.76
  304.6 5.9 fusion.211
  313.0 7.0 fusion.91
  320.0 4.5 fusion.78
  325.3 24.8 %fusion.9 = (f32[8,256,6]{1,2,0:T(8,128)}, f32[8,256,6]{1,2,0:T(8,128)}, f32[8,256,6]{1,2,0:T(8,128)}, f32[8,256,256]{2,1,0:T(8,128)S(1)}) fusion(f32[8,256,6]{1,2,0:T(8,128)} %bitcast.330, f32[8,256,6]{1,2,0:T(8,128)} %copy.199, f32[8,256,256]{2,1,0:T(8,128)} %copy-done.32, pred[256,256]{1,0:T(8,128)(4,1)} %iota_compare_fusion, ...), kind=kOutput, calls=%fused_computation.14 | convolution fusion | flops 2462543872 | bytes 10797056 | tf_op jit(solution)/shard_map/transpose(jvp(ctsh,cshp->cthp))/dot_general | solution.py:44
  350.0 3.5 convolution_add_fusion.2
  359.2 14.2 %bitcast_add_fusion.1 = f32[8,256,6,64]{1,3,2,0:T(8,128)S(1)} fusion(f32[8,256,6,64]{1,3,2,0:T(8,128)} %fusion.78, f32[8,256,6]{1,2,0:T(8,128)} %bitcast.331, f32[8,256,6]{1,2,0:T(8,128)} %copy.199, f32[8,256,256]{2,1,0:T(8,128)} %copy-done.32, pred[256,256]{1,0:T(8,128)(4,1)} %iota_compare_fusion, f32[8,6,64,256]{3,0,2,1:T(8,128)} %bitcast.304, ...), kind=kOutput, calls=%fused_computation.43 | convolution fusion | flops 2433220608 | bytes 11747328 | tf_op jit(solution)/shard_map/transpose(jvp(ctsh,cshp->cthp))/dot_general | solution.py:44
  375.1 3.1 copy.275
  378.3 3.7 copy.222
  382.1 3.8 multiply_reduce_fusion.1
  387.8 4.3 multiply_reduce_fusion.2
  394.0 3.2 broadcast_multiply_fusion
  402.2 4.0 fusion.224
  406.2 3.8 bitcast_add_fusion
  420.0 4.5 fusion.222
  428.5 50.1 %reduce-scatter.10.cloned.1.call-done = f32[512,768]{1,0:T(8,128)} async-done(((f32[2048,768]{1,0:T(8,128)}), f32[512,768]{1,0:T(8,128)}) %reduce-scatter.10.cloned.1.call-update) | async-done | bytes 1572880 | tf_op jit(solution)/shard_map/reduce_scatter | solution.py:216
  484.2 6.5 reduce.13
  491.8 5.7 all-to-all-start.1
  497.5 3.9 reduce-scatter.8.cloned.1.call-done
  504.4 70.8 %all-reduce.20.cloned.1.call-done = bf16[8,16,2,384]{3,2,1,0:T(2,128)(2,1)} async-done(((bf16[8,16,2,384]{3,2,1,0:T(2,128)(2,1)}), bf16[8,16,2,384]{3,2,1,0:T(2,128)(2,1)}) %all-reduce.20.cloned.1.call-update) | async-done | bytes 196624 | tf_op jit(solution)/shard_map/psum | solution.py:245
  577.0 58.3 %reduce-scatter.6.cloned.1.call-done = f32[512,768]{1,0:T(8,128)} async-done(((f32[2048,768]{1,0:T(8,128)}), f32[512,768]{1,0:T(8,128)}) %reduce-scatter.6.cloned.1.call-update) | async-done | bytes 1572880 | tf_op jit(solution)/shard_map/reduce_scatter | solution.py:166
  640.6 133.8 %all-reduce.22.cloned.1.call-done = (f32[8,768,16]{1,2,0:T(8,128)}, f32[8,1536,16]{1,2,0:T(8,128)}, f32[8,16,768]{2,1,0:T(8,128)}) async-done(((f32[8,768,16]{1,2,0:T(8,128)}, f32[8,1536,16]{1,2,0:T(8,128)}, f32[8,16,768]{2,1,0:T(8,128)}), (f32[8,768,16]{1,2,0:T(8,128)}, f32[8,1536,16]{1,2,0:T(8,128)}, f32[8,16,768]{2,1,0:T(8,128)})) %all-reduce.22.cloned.1.call-update) | async-done | bytes 1572880 | tf_op jit(solution)/shard_map/psum | solution.py:237
  (340 shorter events, 104.4 us)
Async XLA Ops:
  7.2 156.6 %all-gather.7.cloned.1.call-start = ((), (), s32[]{:S(2)}) async-start(), calls=%async_computation.8 | async-start | bytes 1327104 | tf_op jit(solution)/shard_map/all_gather | solution.py:112
  8.9 157.3 %all-gather.9.cloned.1.call-start = ((), (), s32[]{:S(2)}) async-start(), calls=%async_computation.11 | async-start | bytes 3932160 | tf_op jit(solution)/shard_map/all_gather | solution.py:191
  15.6 9.3 %copy-start.94 = (bf16[768]{0:T(1024)(128)(2,1)S(1)}, bf16[768]{0:T(1024)(128)(2,1)}, u32[]{:S(2)}) copy-start(bf16[768]{0:T(1024)(128)(2,1)} %param.29) | copy-start | bytes 4612
  16.3 37.2 %copy-start.100 = (s32[8]{0:T(128)S(1)}, s32[8]{0:T(128)}, u32[]{:S(2)}) copy-start(s32[8]{0:T(128)} %param.28) | copy-start | bytes 100
  16.3 38.5 %copy-start.97 = (bf16[384]{0:T(512)(128)(2,1)S(1)}, bf16[384]{0:T(512)(128)(2,1)}, u32[]{:S(2)}) copy-start(bf16[384]{0:T(512)(128)(2,1)} %param.40) | copy-start | bytes 2308
  16.3 39.1 %copy-start.98 = (f32[6]{0:T(128)S(1)}, f32[6]{0:T(128)}, u32[]{:S(2)}) copy-start(f32[6]{0:T(128)} %param.39) | copy-start | bytes 76
  16.4 39.8 %copy-start.95 = (bf16[96,6]{0,1:T(8,128)(2,1)S(1)}, bf16[96,6]{0,1:T(8,128)(2,1)}, u32[]{:S(2)}) copy-start(bf16[96,6]{0,1:T(8,128)(2,1)} %param.31) | copy-start | bytes 3460
  16.4 65.9 %copy-start.55 = (bf16[8,16,2,384]{3,2,1,0:T(2,128)(2,1)S(1)}, bf16[8,16,2,384]{3,2,1,0:T(2,128)(2,1)}, u32[]{:S(2)}) copy-start(bf16[8,16,2,384]{3,2,1,0:T(2,128)(2,1)} %param.43) | copy-start | bytes 589828
  16.4 66.7 %copy-start.56 = (bf16[8,768,16]{1,2,0:T(8,128)(2,1)S(1)}, bf16[8,768,16]{1,2,0:T(8,128)(2,1)}, u32[]{:S(2)}) copy-start(bf16[8,768,16]{1,2,0:T(8,128)(2,1)} %param.42) | copy-start | bytes 589828
  17.4 66.1 %copy-start.48 = (bf16[8,1536,16]{1,2,0:T(8,128)(2,1)S(1)}, bf16[8,1536,16]{1,2,0:T(8,128)(2,1)}, u32[]{:S(2)}) copy-start(bf16[8,1536,16]{1,2,0:T(8,128)(2,1)} %param.44) | copy-start | bytes 1179652
  17.4 67.4 %copy-start.57 = (bf16[8,16,768]{2,1,0:T(8,128)(2,1)S(1)}, bf16[8,16,768]{2,1,0:T(8,128)(2,1)}, u32[]{:S(2)}) copy-start(bf16[8,16,768]{2,1,0:T(8,128)(2,1)} %param.45) | copy-start | bytes 589828
  17.4 67.6 %copy-start.19 = (bf16[512,768]{1,0:T(8,128)(2,1)S(1)}, bf16[512,768]{1,0:T(8,128)(2,1)}, u32[]{:S(2)}) copy-start(bf16[512,768]{1,0:T(8,128)(2,1)} %fusion.62) | copy-start | bytes 2359300
  17.4 34.0 %all-to-all-start = ((bf16[8,1,64,768]{3,2,1,0:T(8,128)(2,1)}), bf16[8,1,64,768]{3,2,1,0:T(8,128)(2,1)S(1)}, u32[]{:S(2)}, u32[]{:S(2)}) async-start(bf16[8,1,64,768]{3,2,1,0:T(8,128)(2,1)} %bitcast_select_fusion.1), calls=%async_computation | async-start | bytes 1572864 | tf_op jit(solution)/shard_map/all_to_all | solution.py:122
  24.8 66.9 %copy-start.90 = (f32[4,384]{1,0:T(4,128)S(1)}, f32[4,384]{1,0:T(4,128)}, u32[]{:S(2)}) copy-start(f32[4,384]{1,0:T(4,128)} %param.33) | copy-start | bytes 18436
  24.8 146.8 %all-gather.5.cloned.1.call-start = ((), (), s32[]{:S(2)}) async-start(), calls=%async_computation.7 | async-start | bytes 3932160 | tf_op jit(solution)/shard_map/all_gather | solution.py:146
  24.9 26.9 %copy-start.66 = (f32[768]{0:T(1024)}, f32[768]{0:T(1024)S(1)}, u32[]{:S(2)}) copy-start(f32[768]{0:T(1024)S(1)} %convert_element_type.111) | copy-start | bytes 9220
  51.5 40.9 %copy-start.5 = (bf16[8,1,64,768]{3,2,1,0:T(8,128)(2,1)}, bf16[8,1,64,768]{3,2,1,0:T(8,128)(2,1)S(1)}, u32[]{:S(2)}) copy-start(bf16[8,1,64,768]{3,2,1,0:T(8,128)(2,1)S(1)} %all-to-all-done) | copy-start | bytes 2359300
  51.7 73.8 %copy-start.91 = (f32[4,256]{1,0:T(4,128)S(1)}, f32[4,256]{1,0:T(4,128)}, u32[]{:S(2)}) copy-start(f32[4,256]{1,0:T(4,128)} %param.35) | copy-start | bytes 12292
  53.5 104.2 %copy-start.21 = (bf16[512,768]{1,0:T(8,128)(2,1)S(1)}, bf16[512,768]{1,0:T(8,128)(2,1)}, u32[]{:S(2)}) copy-start(bf16[512,768]{1,0:T(8,128)(2,1)} %fusion.67) | copy-start | bytes 2359300
  53.5 373.6 %reduce-scatter.12.cloned.1.call-start = ((), (), s32[]{:S(2)}) async-start(), calls=%async_computation.13 | async-start | bytes 2621440 | tf_op jit(solution)/shard_map/reduce_scatter | solution.py:218
  83.5 82.7 %copy-start.37 = (bf16[1,768,16]{2,1,0:T(8,128)(2,1)}, bf16[1,768,16]{2,1,0:T(8,128)(2,1)S(1)}, u32[]{:S(2)}) copy-start(bf16[1,768,16]{2,1,0:T(8,128)(2,1)S(1)} %copy.244) | copy-start | bytes 73732
  85.0 40.4 %copy-start.53 = (bf16[1,16,768]{2,0,1:T(2,128)(2,1)}, bf16[1,16,768]{2,0,1:T(2,128)(2,1)S(1)}, u32[]{:S(2)}) copy-start(bf16[1,16,768]{2,0,1:T(2,128)(2,1)S(1)} %fusion.135) | copy-start | bytes 73732
  157.7 14.0 %copy-start.30 = (bf16[384,768]{0,1:T(8,128)(2,1)}, bf16[384,768]{0,1:T(8,128)(2,1)S(1)}, u32[]{:S(2)}) copy-start(bf16[384,768]{0,1:T(8,128)(2,1)S(1)} %all_gather.29) | copy-start | bytes 1769476
  171.6 14.5 %copy-start.3 = (bf16[2048,768]{1,0:T(8,128)(2,1)S(1)}, bf16[2048,768]{1,0:T(8,128)(2,1)}, u32[]{:S(2)}) copy-start(bf16[2048,768]{1,0:T(8,128)(2,1)} %all-gather.5.cloned.1.call-done) | copy-start | bytes 9437188
  220.5 9.4 %copy-start.32 = (f32[8,256,256]{2,1,0:T(8,128)}, f32[8,256,256]{2,1,0:T(8,128)S(1)}, u32[]{:S(2)}) copy-start(f32[8,256,256]{2,1,0:T(8,128)S(1)} %fusion.221) | copy-start | bytes 6291460
  229.9 15.4 %copy-start.23 = (f32[8,256,6,64]{1,3,2,0:T(8,128)}, f32[8,256,6,64]{1,3,2,0:T(8,128)S(1)}, u32[]{:S(2)}) copy-start(f32[8,256,6,64]{1,3,2,0:T(8,128)S(1)} %fusion.84) | copy-start | bytes 9437188
  293.7 26.3 %copy-start.2 = (f32[48,8,8,256]{3,2,1,0:T(8,128)}, f32[48,8,8,256]{3,2,1,0:T(8,128)S(1)}, u32[]{:S(2)}) copy-start(f32[48,8,8,256]{3,2,1,0:T(8,128)S(1)} %copy.274) | copy-start | bytes 9437188
  325.3 24.8 %copy-start.14 = (f32[2048,128]{1,0:T(8,128)S(1)}, f32[2048,128]{1,0:T(8,128)}, u32[]{:S(2)}) copy-start(f32[2048,128]{1,0:T(8,128)} %get-tuple-element.90) | copy-start | bytes 3145732
  325.3 24.8 %copy-start.28 = (f32[8,256,128]{2,1,0:T(8,128)S(1)}, f32[8,256,128]{2,1,0:T(8,128)}, u32[]{:S(2)}) copy-start(f32[8,256,128]{2,1,0:T(8,128)} %fusion.91) | copy-start | bytes 3145732
  359.1 69.4 %reduce-scatter.14.cloned.1.call-start = ((), (), s32[]{:S(2)}) async-start(), calls=%async_computation.14 | async-start | bytes 163840 | tf_op jit(solution)/shard_map/reduce_scatter | solution.py:217
  402.1 76.5 %reduce-scatter.10.cloned.1.call-start = ((), (), s32[]{:S(2)}) async-start(), calls=%async_computation.12 | async-start | bytes 7864320 | tf_op jit(solution)/shard_map/reduce_scatter | solution.py:216
  410.0 91.3 %reduce-scatter.8.cloned.1.call-start = ((), (), s32[]{:S(2)}) async-start(), calls=%async_computation.10 | async-start | bytes 163840 | tf_op jit(solution)/shard_map/reduce_scatter | solution.py:172
  415.8 159.3 %all-reduce.20.cloned.1.call-start = ((), (), s32[]{:S(2)}) async-start(), calls=%async_computation.15 | async-start | bytes 393216 | tf_op jit(solution)/shard_map/psum | solution.py:245
  419.9 215.4 %reduce-scatter.6.cloned.1.call-start = ((), (), s32[]{:S(2)}) async-start(), calls=%async_computation.9 | async-start | bytes 7864320 | tf_op jit(solution)/shard_map/reduce_scatter | solution.py:166
  425.1 53.5 %copy-start.6 = (bf16[8,1,64,768]{3,2,1,0:T(8,128)(2,1)S(1)}, bf16[8,1,64,768]{3,2,1,0:T(8,128)(2,1)}, u32[]{:S(2)}) copy-start(bf16[8,1,64,768]{3,2,1,0:T(8,128)(2,1)} %copy-done.5) | copy-start | bytes 2359300
  425.1 53.5 %copy-start.67 = (f32[768]{0:T(1024)S(1)}, f32[768]{0:T(1024)}, u32[]{:S(2)}) copy-start(f32[768]{0:T(1024)} %copy-done.66) | copy-start | bytes 9220
  428.5 52.3 %copy-start.29 = (bf16[1,512,768]{2,1,0:T(8,128)(2,1)S(1)}, bf16[1,512,768]{2,1,0:T(8,128)(2,1)}, u32[]{:S(2)}) copy-start(bf16[1,512,768]{2,1,0:T(8,128)(2,1)} %param.25) | copy-start | bytes 2359300
  483.7 17.7 %copy-start.20 = (bf16[512,768]{1,0:T(8,128)(2,1)S(1)}, bf16[512,768]{1,0:T(8,128)(2,1)}, u32[]{:S(2)}) copy-start(bf16[512,768]{1,0:T(8,128)(2,1)} %fusion.62) | copy-start | bytes 2359300
  484.2 19.0 %copy-start.22 = (bf16[512,768]{1,0:T(8,128)(2,1)S(1)}, bf16[512,768]{1,0:T(8,128)(2,1)}, u32[]{:S(2)}) copy-start(bf16[512,768]{1,0:T(8,128)(2,1)} %fusion.67) | copy-start | bytes 2359300
  484.2 19.0 %copy-start.58 = (f32[512,16]{0,1:T(8,128)S(1)}, f32[512,16]{0,1:T(8,128)}, u32[]{:S(2)}) copy-start(f32[512,16]{0,1:T(8,128)} %reduce-scatter.14.cloned.1.call-done) | copy-start | bytes 98308
  491.7 12.6 %copy-start.99 = (s32[8]{0:T(128)S(1)}, s32[8]{0:T(128)}, u32[]{:S(2)}) copy-start(s32[8]{0:T(128)} %compare_select_fusion.3) | copy-start | bytes 100
  491.7 12.6 %copy-start.102 = (s32[8]{0:T(128)S(1)}, s32[8]{0:T(128)}, u32[]{:S(2)}) copy-start(s32[8]{0:T(128)} %param.27) | copy-start | bytes 100
  491.7 143.6 %copy-start.54 = (bf16[1,16,768]{2,0,1:T(2,128)(2,1)S(1)}, bf16[1,16,768]{2,0,1:T(2,128)(2,1)}, u32[]{:S(2)}) copy-start(bf16[1,16,768]{2,0,1:T(2,128)(2,1)} %copy-done.53) | copy-start | bytes 73732
  491.8 143.6 %copy-start.78 = (f32[512]{0:T(512)S(1)}, f32[512]{0:T(512)}, u32[]{:S(2)}) copy-start(f32[512]{0:T(512)} %copy-done.77) | copy-start | bytes 6148
  491.8 146.3 %all-to-all-start.1 = ((bf16[8,2,24576]{2,1,0:T(2,128)(2,1)}), bf16[8,2,24576]{2,1,0:T(2,128)(2,1)S(1)}, u32[]{:S(2)}, u32[]{:S(2)}) async-start(bf16[8,2,24576]{2,1,0:T(2,128)(2,1)} %reshape.388), calls=%async_computation.6 | async-start | bytes 1572864 | tf_op jit(solution)/shard_map/all_to_all | solution.py:235
  497.4 277.0 %all-reduce.22.cloned.1.call-start = ((), (), s32[]{:S(2)}) async-start(), calls=%async_computation.16 | async-start | bytes 3145728 | tf_op jit(solution)/shard_map/psum | solution.py:237
  501.3 134.0 %copy-start.59 = (f32[512,16]{0,1:T(8,128)S(1)}, f32[512,16]{0,1:T(8,128)}, u32[]{:S(2)}) copy-start(f32[512,16]{0,1:T(8,128)} %reduce-scatter.8.cloned.1.call-done) | copy-start | bytes 98308
  639.0 141.0 %copy-start.1 = (bf16[8,1,64,768]{3,2,1,0:T(8,128)(2,1)S(1)}, bf16[8,1,64,768]{3,2,1,0:T(8,128)(2,1)}, u32[]{:S(2)}) copy-start(bf16[8,1,64,768]{3,2,1,0:T(8,128)(2,1)} %param.24) | copy-start | bytes 2359300
  (67 other events, 231.7 us)
Sparse Core Ops, SparseCore 0:
  10.8 49.3 all-gather.6
  62.3 27.2 all-gather.8
  91.8 28.8 all-gather.4
  359.2 27.7 reduce-scatter.11
  402.2 15.5 reduce-scatter.13
  420.2 58.3 reduce-scatter.9
  481.7 19.5 reduce-scatter.7
  504.6 70.4 all-reduce.19
  577.9 57.4 reduce-scatter.5
  641.4 132.9 all-reduce.21
where the time goes:
time: 792 us; the launch traced here: 787 us
  waiting for transfers between devices  344 us (43%)
  matrix products  158 us (20%)
  blocking collectives  113 us (14%)
  local copies, waits for them, and re-layouts  83.5 us (11%)
  other arithmetic  56.7 us (7%)
  between operations  18 us (2%)
  starting transfers between devices  13.7 us (2%)
    psum x1, waiting for transfers between devices, shards(): lax.psum((chosen[:, None, None] * indown_sum[None], chosen[:, None, None]...  134 us
    psum x1, waiting for transfers between devices, shards(): lax.psum((chosen[:, None, None, None] * inup_sum[None]).astype(jnp.bfloat...  70.8 us
    reduce_scatter x1, waiting for transfers between devices, shards(): lax.psum_scatter(jnp.dot(normed_out, full_out, preferred_element_type=jnp...  58.3 us
    dot_general x3, matrix products, state_mixer(): inside = jnp.einsum('ctsh,cshp->cthp', weights, block_x, precision=HIGHEST)  54.3 us
    reduce_scatter x1, waiting for transfers between devices, shards(): lax.psum_scatter(normed_part, 'tensor', scatter_dimension=0, tiled=True)  50.1 us
    unnamed x223, local copies, waits for them, and re-layouts  36.8 us
    all_gather x1, blocking collectives, shards(): lax.all_gather(w_out, 'dp', axis=1, tiled=True)  31.6 us
    all_gather x1, blocking collectives, shards(): lax.all_gather(w_bc, 'dp', axis=0, tiled=True)  31.3 us
  transfers between devices with their start and end apart: 12, of which 6 were waited for; matrix products, arithmetic and copies ran while one was open for 14% of the time, Pallas kernels for 0%

commit v1 on v0

--- a/solution.py
+++ b/solution.py
@@ -3,12 +3,25 @@
 import jax.numpy as jnp
 from jax import lax
 from jax.sharding import PartitionSpec as P
+from jax.lax import all_to_all, axis_size
 
 INNER = 1536
 SPAN = 256
 ADAPTERS = 8
 EPSILON = 1e-05
 HIGHEST = lax.Precision.HIGHEST
+
+
+def produce_heaps(u):
+    return jnp.concatenate(
+        all_to_all(
+            jnp.stack(jnp.split(u, axis_size("dp"), axis=0), axis=0),
+            concat_axis=0,
+            axis_name="dp",
+            split_axis=0,
+        ),
+        axis=2,
+    )
 
 
 def causal_conv(values, kernel, offsets):
@@ -119,7 +132,7 @@
     placed = (dealt_to[None, :] == slot_ids[:, None]).astype(jnp.int32)
     seq_of = jnp.sum(placed * slot_ids[None, :], axis=1)
     picked = jnp.take(tokens, seq_of, axis=0)
-    arrived = lax.all_to_all(picked, "dp", split_axis=0, concat_axis=2, tiled=True)
+    arrived = produce_heaps(picked)
     tok_rows = arrived.reshape(-1, model_dim)
     tok_dev = tok_rows.shape[0]
     group_id = lax.axis_index("dp")

time: 792 us -> 802 us (1.013)
    unnamed x223 -> x228, local copies, waits for them, and re-layouts: 36.8 us -> 41.5 us
  transfers between devices with their start and end apart: 12 -> 12, of which waited for: 6 -> 6; matrix products, arithmetic and copies ran while one was open for 14% -> 15% of each run, Pallas kernels for 0% -> 0%
where the time goes in v1:
time: 802 us; the launch traced here: 796 us
  waiting for transfers between devices  347 us (43%)
  matrix products  158 us (20%)
  blocking collectives  113 us (14%)
  local copies, waits for them, and re-layouts  88.8 us (11%)
  other arithmetic  57.3 us (7%)
  between operations  17.9 us (2%)
  starting transfers between devices  13.7 us (2%)
    psum x1, waiting for transfers between devices, shards(): lax.psum((chosen[:, None, None] * indown_sum[None], chosen[:, None, None]...  134 us
    psum x1, waiting for transfers between devices, shards(): lax.psum((chosen[:, None, None, None] * inup_sum[None]).astype(jnp.bfloat...  70.8 us
    reduce_scatter x1, waiting for transfers between devices, shards(): lax.psum_scatter(jnp.dot(normed_out, full_out, preferred_element_type=jnp...  58.3 us
    dot_general x3, matrix products, state_mixer(): inside = jnp.einsum('ctsh,cshp->cthp', weights, block_x, precision=HIGHEST)  54.3 us
    reduce_scatter x1, waiting for transfers between devices, shards(): lax.psum_scatter(normed_part, 'tensor', scatter_dimension=0, tiled=True)  50.4 us
    unnamed x228, local copies, waits for them, and re-layouts  41.5 us
    all_gather x1, blocking collectives, shards(): lax.all_gather(w_out, 'dp', axis=1, tiled=True)  31.6 us
    all_gather x1, blocking collectives, shards(): lax.all_gather(w_bc, 'dp', axis=0, tiled=True)  31.3 us
  transfers between devices with their start and end apart: 12, of which 6 were waited for; matrix products, arithmetic and copies ran while one was open for 15% of the time, Pallas kernels for 0%

profile of v1, /device:TPU:0, one launch (start us, length us, event | category | flops | bytes accessed | tf_op | source)
XLA Modules:
  0.0 796.4 jit_solution(10344706451945506515)
XLA Ops:
  23.0 7.4 all-to-all-start
  30.5 29.6 %all-to-all-done = bf16[8,1,1,64,768]{4,3,2,1,0:T(8,128)(2,1)S(1)} async-done(((bf16[8,1,1,64,768]{4,3,2,1,0:T(8,128)(2,1)}), bf16[8,1,1,64,768]{4,3,2,1,0:T(8,128)(2,1)S(1)}, u32[]{:S(2)}, u32[]{:S(2)}) %all-to-all-start) | async-done | bytes 786464 | tf_op jit(solution)/shard_map/all_to_all | solution.py:17
  64.7 26.0 %all-gather = bf16[8,96,6]{1,2,0:T(8,128)(2,1)S(1)} all-gather(bf16[1,96,6]{1,2,0:T(8,128)(2,1)S(1)} %bitcast.395), channel_id=1, replica_groups=mesh['dp'=8,'tensor'=4] {'dp'}, dimensions={0}, use_global_device_ids=true | all-gather | bytes 10368 | tf_op jit(solution)/shard_map/all_gather | solution.py:126
  93.9 5.8 all_gather.31
  101.5 31.3 %all_gather.27 = bf16[768,256]{1,0:T(8,128)(2,1)S(1)} all-gather(bf16[96,256]{1,0:T(8,128)(2,1)} %param.32), channel_id=1, replica_groups=mesh['dp'=8,'tensor'=4] {'dp'}, dimensions={0}, use_global_device_ids=true | all-gather | bytes 442368 | tf_op jit(solution)/shard_map/all_gather | solution.py:127
  134.7 31.6 %all_gather.29 = bf16[384,768]{0,1:T(8,128)(2,1)S(1)} all-gather(bf16[384,96]{0,1:T(8,128)(2,1)} %param.41), channel_id=1, replica_groups=mesh['dp'=8,'tensor'=4] {'dp'}, dimensions={1}, use_global_device_ids=true | all-gather | bytes 663552 | tf_op jit(solution)/shard_map/all_gather | solution.py:128
  166.6 5.9 all_gather.26
  174.8 5.4 fusion.231
  180.2 3.6 compare_select_fusion.2
  194.8 3.9 fusion.227
  199.8 3.0 fusion.223
  202.8 3.6 copy.303
  211.5 3.8 copy.304
  215.4 4.4 fusion.33
  219.7 4.0 copy.232
  223.7 3.5 copy.306
  229.1 3.8 fusion.41
  235.4 3.0 fusion.84
  238.5 15.3 %bitcast_add_fusion.2 = f32[8,256,6,64]{1,3,2,0:T(8,128)S(1)} fusion(f32[8,256,6,64]{1,3,2,0:T(8,128)S(1)} %fusion.84, f32[8,256,6]{1,2,0:T(8,128)S(1)} %bitcast.374, f32[8,256,6]{1,2,0:T(8,128)S(1)} %copy-done.64, f32[8,256,256]{2,1,0:T(8,128)S(1)} %fusion.229, pred[256,256]{1,0:T(8,128)(4,1)S(1)} %copy-done.65, f32[8,256,6,64]{1,0,3,2:T(8,128)S(1)} %bitcast.339, ...), kind=kOutput, calls=%fused_computation.50 | convolution fusion | flops 2433220608 | bytes 11747328 | tf_op jit(solution)/shard_map/jvp(ctsh,cshp->cthp)/dot_general | solution.py:57
  258.7 3.6 copy.248
  262.3 10.0 %multiply_reduce_fusion.3 = (f32[2048]{0:T(1024)}, f32[2048]{0:T(1024)}, f32[2048,384]{1,0:T(8,128)}, f32[2048,384]{1,0:T(8,128)}) fusion(f32[2048,1,384]{2,0,1:T(8,128)} %copy.304, f32[2048,384]{1,0:T(8,128)} %copy.248, f32[2048,384]{1,0:T(8,128)} %get-tuple-element.75, f32[384]{0:T(512)} %mul.549, f32[2048,384]{1,0:T(8,128)} %fusion.231, ...), kind=kOutput, calls=%fused_computation.55 | convolution fusion | flops 38531072 | bytes 19058692 | tf_op jit(solution)/shard_map/dot_general | solution.py:207
  272.2 12.8 %all-reduce.16 = (f32[2048]{0:T(1024)}, f32[2048]{0:T(1024)}) all-reduce(f32[2048]{0:T(1024)} %get-tuple-element.57, f32[2048]{0:T(1024)} %get-tuple-element.56), channel_id=1, replica_groups=mesh['dp'=8,'tensor'=4] {'tensor'}, use_global_device_ids=true, to_apply=%region_3.5 | all-reduce | flops 4096 | bytes 32768 | tf_op jit(solution)/shard_map/psum | solution.py:173
  286.4 9.0 %fusion.24 = (f32[2048,1,384]{2,0,1:T(8,128)}, f32[2048,384]{1,0:T(8,128)}, bf16[2048,384]{1,0:T(8,128)(2,1)}) fusion(f32[2048,1,384]{2,0,1:T(8,128)} %copy.304, f32[2048]{0:T(1024)S(1)} %broadcast_multiply_fusion.11, f32[2048,384]{1,0:T(8,128)} %get-tuple-element.73, f32[2048]{0:T(1024)S(1)} %get-tuple-element.93, f32[2048,384]{1,0:T(8,128)} %get-tuple-element.103, ...), kind=kLoop, calls=%fused_computation.34 | loop fusion | flops 19660800 | bytes 23620608 | tf_op jit(solution)/shard_map/transpose(jvp())/broadcast_in_dim | solution.py:95
  295.4 4.0 copy.250
  299.4 3.4 copy.309
  302.8 7.0 fusion.88
  309.9 3.8 fusion.76
  313.7 5.9 fusion.219
  322.1 7.0 fusion.91
  329.1 4.5 fusion.78
  334.4 24.8 %fusion.9 = (f32[8,256,6]{1,2,0:T(8,128)}, f32[8,256,6]{1,2,0:T(8,128)}, f32[8,256,6]{1,2,0:T(8,128)}, f32[8,256,256]{2,1,0:T(8,128)S(1)}) fusion(f32[8,256,6]{1,2,0:T(8,128)} %bitcast.372, f32[8,256,6]{1,2,0:T(8,128)} %copy.234, f32[8,256,256]{2,1,0:T(8,128)} %copy-done.32, pred[256,256]{1,0:T(8,128)(4,1)} %iota_compare_fusion, ...), kind=kOutput, calls=%fused_computation.14 | convolution fusion | flops 2462543872 | bytes 10797056 | tf_op jit(solution)/shard_map/transpose(jvp(ctsh,cshp->cthp))/dot_general | solution.py:57
  359.1 3.5 convolution_add_fusion.2
  368.3 14.2 %bitcast_add_fusion.1 = f32[8,256,6,64]{1,3,2,0:T(8,128)S(1)} fusion(f32[8,256,6,64]{1,3,2,0:T(8,128)} %fusion.78, f32[8,256,6]{1,2,0:T(8,128)} %bitcast.373, f32[8,256,6]{1,2,0:T(8,128)} %copy.234, f32[8,256,256]{2,1,0:T(8,128)} %copy-done.32, pred[256,256]{1,0:T(8,128)(4,1)} %iota_compare_fusion, f32[8,6,64,256]{3,0,2,1:T(8,128)} %bitcast.346, ...), kind=kOutput, calls=%fused_computation.43 | convolution fusion | flops 2433220608 | bytes 11747328 | tf_op jit(solution)/shard_map/transpose(jvp(ctsh,cshp->cthp))/dot_general | solution.py:57
  384.2 3.1 copy.310
  387.4 3.7 copy.257
  391.2 3.8 multiply_reduce_fusion.1
  396.9 4.3 multiply_reduce_fusion.2
  403.1 3.2 broadcast_multiply_fusion
  411.3 4.0 fusion.232
  415.3 3.8 bitcast_add_fusion
  429.1 4.5 fusion.230
  437.3 50.4 %reduce-scatter.10.cloned.1.call-done = f32[512,768]{1,0:T(8,128)} async-done(((f32[2048,768]{1,0:T(8,128)}), f32[512,768]{1,0:T(8,128)}) %reduce-scatter.10.cloned.1.call-update) | async-done | bytes 1572880 | tf_op jit(solution)/shard_map/reduce_scatter | solution.py:229
  493.3 6.5 reduce.12
  500.9 5.7 all-to-all-start.1
  506.6 3.9 reduce-scatter.8.cloned.1.call-done
  513.5 70.8 %all-reduce.20.cloned.1.call-done = bf16[8,16,2,384]{3,2,1,0:T(2,128)(2,1)} async-done(((bf16[8,16,2,384]{3,2,1,0:T(2,128)(2,1)}), bf16[8,16,2,384]{3,2,1,0:T(2,128)(2,1)}) %all-reduce.20.cloned.1.call-update) | async-done | bytes 196624 | tf_op jit(solution)/shard_map/psum | solution.py:258
  586.1 58.3 %reduce-scatter.6.cloned.1.call-done = f32[512,768]{1,0:T(8,128)} async-done(((f32[2048,768]{1,0:T(8,128)}), f32[512,768]{1,0:T(8,128)}) %reduce-scatter.6.cloned.1.call-update) | async-done | bytes 1572880 | tf_op jit(solution)/shard_map/reduce_scatter | solution.py:179
  649.7 133.8 %all-reduce.22.cloned.1.call-done = (f32[8,768,16]{1,2,0:T(8,128)}, f32[8,1536,16]{1,2,0:T(8,128)}, f32[8,16,768]{2,1,0:T(8,128)}) async-done(((f32[8,768,16]{1,2,0:T(8,128)}, f32[8,1536,16]{1,2,0:T(8,128)}, f32[8,16,768]{2,1,0:T(8,128)}), (f32[8,768,16]{1,2,0:T(8,128)}, f32[8,1536,16]{1,2,0:T(8,128)}, f32[8,16,768]{2,1,0:T(8,128)})) %all-reduce.22.cloned.1.call-update) | async-done | bytes 1572880 | tf_op jit(solution)/shard_map/psum | solution.py:250
  (347 shorter events, 110.4 us)
Async XLA Ops:
  7.2 9.6 %copy-start = (bf16[8,1,64,768]{3,2,1,0:T(8,128)(2,1)S(1)}, bf16[8,1,64,768]{3,2,1,0:T(8,128)(2,1)}, u32[]{:S(2)}) copy-start(bf16[8,1,64,768]{3,2,1,0:T(8,128)(2,1)} %param.24) | copy-start | bytes 2359300
  7.2 165.3 %all-gather.7.cloned.1.call-start = ((), (), s32[]{:S(2)}) async-start(), calls=%async_computation.8 | async-start | bytes 1327104 | tf_op jit(solution)/shard_map/all_gather | solution.py:125
  8.9 165.9 %all-gather.9.cloned.1.call-start = ((), (), s32[]{:S(2)}) async-start(), calls=%async_computation.11 | async-start | bytes 3932160 | tf_op jit(solution)/shard_map/all_gather | solution.py:204
  17.4 13.0 %copy-start.94 = (bf16[768]{0:T(1024)(128)(2,1)S(1)}, bf16[768]{0:T(1024)(128)(2,1)}, u32[]{:S(2)}) copy-start(bf16[768]{0:T(1024)(128)(2,1)} %param.29) | copy-start | bytes 4612
  22.1 40.0 %copy-start.101 = (s32[8]{0:T(128)S(1)}, s32[8]{0:T(128)}, u32[]{:S(2)}) copy-start(s32[8]{0:T(128)} %param.28) | copy-start | bytes 100
  22.1 41.2 %copy-start.98 = (bf16[384]{0:T(512)(128)(2,1)S(1)}, bf16[384]{0:T(512)(128)(2,1)}, u32[]{:S(2)}) copy-start(bf16[384]{0:T(512)(128)(2,1)} %param.40) | copy-start | bytes 2308
  22.1 41.8 %copy-start.99 = (f32[6]{0:T(128)S(1)}, f32[6]{0:T(128)}, u32[]{:S(2)}) copy-start(f32[6]{0:T(128)} %param.39) | copy-start | bytes 76
  22.1 42.6 %copy-start.95 = (bf16[96,6]{0,1:T(8,128)(2,1)S(1)}, bf16[96,6]{0,1:T(8,128)(2,1)}, u32[]{:S(2)}) copy-start(bf16[96,6]{0,1:T(8,128)(2,1)} %param.31) | copy-start | bytes 3460
  22.1 68.7 %copy-start.55 = (bf16[8,16,2,384]{3,2,1,0:T(2,128)(2,1)S(1)}, bf16[8,16,2,384]{3,2,1,0:T(2,128)(2,1)}, u32[]{:S(2)}) copy-start(bf16[8,16,2,384]{3,2,1,0:T(2,128)(2,1)} %param.43) | copy-start | bytes 589828
  22.1 69.5 %copy-start.56 = (bf16[8,768,16]{1,2,0:T(8,128)(2,1)S(1)}, bf16[8,768,16]{1,2,0:T(8,128)(2,1)}, u32[]{:S(2)}) copy-start(bf16[8,768,16]{1,2,0:T(8,128)(2,1)} %param.42) | copy-start | bytes 589828
  22.3 69.8 %copy-start.48 = (bf16[8,1536,16]{1,2,0:T(8,128)(2,1)S(1)}, bf16[8,1536,16]{1,2,0:T(8,128)(2,1)}, u32[]{:S(2)}) copy-start(bf16[8,1536,16]{1,2,0:T(8,128)(2,1)} %param.44) | copy-start | bytes 1179652
  23.0 70.4 %copy-start.57 = (bf16[8,16,768]{2,1,0:T(8,128)(2,1)S(1)}, bf16[8,16,768]{2,1,0:T(8,128)(2,1)}, u32[]{:S(2)}) copy-start(bf16[8,16,768]{2,1,0:T(8,128)(2,1)} %param.45) | copy-start | bytes 589828
  23.0 70.6 %copy-start.19 = (bf16[512,768]{1,0:T(8,128)(2,1)S(1)}, bf16[512,768]{1,0:T(8,128)(2,1)}, u32[]{:S(2)}) copy-start(bf16[512,768]{1,0:T(8,128)(2,1)} %fusion.62) | copy-start | bytes 2359300
  23.0 37.1 %all-to-all-start = ((bf16[8,1,1,64,768]{4,3,2,1,0:T(8,128)(2,1)}), bf16[8,1,1,64,768]{4,3,2,1,0:T(8,128)(2,1)S(1)}, u32[]{:S(2)}, u32[]{:S(2)}) async-start(bf16[8,1,1,64,768]{4,3,2,1,0:T(8,128)(2,1)} %fusion.141), calls=%async_computation | async-start | bytes 1572864 | tf_op jit(solution)/shard_map/all_to_all | solution.py:17
  30.4 69.9 %copy-start.90 = (f32[4,384]{1,0:T(4,128)S(1)}, f32[4,384]{1,0:T(4,128)}, u32[]{:S(2)}) copy-start(f32[4,384]{1,0:T(4,128)} %param.33) | copy-start | bytes 18436
  30.4 149.8 %all-gather.5.cloned.1.call-start = ((), (), s32[]{:S(2)}) async-start(), calls=%async_computation.7 | async-start | bytes 3932160 | tf_op jit(solution)/shard_map/all_gather | solution.py:159
  30.5 29.9 %copy-start.66 = (f32[768]{0:T(1024)}, f32[768]{0:T(1024)S(1)}, u32[]{:S(2)}) copy-start(f32[768]{0:T(1024)S(1)} %convert_element_type.108) | copy-start | bytes 9220
  60.0 40.9 %copy-start.5 = (bf16[8,1,1,64,768]{4,3,2,1,0:T(8,128)(2,1)}, bf16[8,1,1,64,768]{4,3,2,1,0:T(8,128)(2,1)S(1)}, u32[]{:S(2)}) copy-start(bf16[8,1,1,64,768]{4,3,2,1,0:T(8,128)(2,1)S(1)} %all-to-all-done) | copy-start | bytes 2359300
  60.3 73.8 %copy-start.91 = (f32[4,256]{1,0:T(4,128)S(1)}, f32[4,256]{1,0:T(4,128)}, u32[]{:S(2)}) copy-start(f32[4,256]{1,0:T(4,128)} %param.35) | copy-start | bytes 12292
  62.0 104.2 %copy-start.21 = (bf16[512,768]{1,0:T(8,128)(2,1)S(1)}, bf16[512,768]{1,0:T(8,128)(2,1)}, u32[]{:S(2)}) copy-start(bf16[512,768]{1,0:T(8,128)(2,1)} %fusion.67) | copy-start | bytes 2359300
  62.1 373.7 %reduce-scatter.12.cloned.1.call-start = ((), (), s32[]{:S(2)}) async-start(), calls=%async_computation.13 | async-start | bytes 2621440 | tf_op jit(solution)/shard_map/reduce_scatter | solution.py:231
  92.1 82.7 %copy-start.37 = (bf16[1,768,16]{2,1,0:T(8,128)(2,1)}, bf16[1,768,16]{2,1,0:T(8,128)(2,1)S(1)}, u32[]{:S(2)}) copy-start(bf16[1,768,16]{2,1,0:T(8,128)(2,1)S(1)} %copy.279) | copy-start | bytes 73732
  93.6 40.5 %copy-start.53 = (bf16[1,16,768]{2,0,1:T(2,128)(2,1)}, bf16[1,16,768]{2,0,1:T(2,128)(2,1)S(1)}, u32[]{:S(2)}) copy-start(bf16[1,16,768]{2,0,1:T(2,128)(2,1)S(1)} %fusion.135) | copy-start | bytes 73732
  166.3 14.0 %copy-start.30 = (bf16[384,768]{0,1:T(8,128)(2,1)}, bf16[384,768]{0,1:T(8,128)(2,1)S(1)}, u32[]{:S(2)}) copy-start(bf16[384,768]{0,1:T(8,128)(2,1)S(1)} %all_gather.29) | copy-start | bytes 1769476
  180.2 14.5 %copy-start.3 = (bf16[2048,768]{1,0:T(8,128)(2,1)S(1)}, bf16[2048,768]{1,0:T(8,128)(2,1)}, u32[]{:S(2)}) copy-start(bf16[2048,768]{1,0:T(8,128)(2,1)} %all-gather.5.cloned.1.call-done) | copy-start | bytes 9437188
  238.5 15.4 %copy-start.23 = (f32[8,256,6,64]{1,3,2,0:T(8,128)}, f32[8,256,6,64]{1,3,2,0:T(8,128)S(1)}, u32[]{:S(2)}) copy-start(f32[8,256,6,64]{1,3,2,0:T(8,128)S(1)} %fusion.84) | copy-start | bytes 9437188
  302.8 26.3 %copy-start.2 = (f32[48,8,8,256]{3,2,1,0:T(8,128)}, f32[48,8,8,256]{3,2,1,0:T(8,128)S(1)}, u32[]{:S(2)}) copy-start(f32[48,8,8,256]{3,2,1,0:T(8,128)S(1)} %copy.309) | copy-start | bytes 9437188
  334.4 24.8 %copy-start.14 = (f32[2048,128]{1,0:T(8,128)S(1)}, f32[2048,128]{1,0:T(8,128)}, u32[]{:S(2)}) copy-start(f32[2048,128]{1,0:T(8,128)} %get-tuple-element.90) | copy-start | bytes 3145732
  334.4 24.8 %copy-start.28 = (f32[8,256,128]{2,1,0:T(8,128)S(1)}, f32[8,256,128]{2,1,0:T(8,128)}, u32[]{:S(2)}) copy-start(f32[8,256,128]{2,1,0:T(8,128)} %fusion.91) | copy-start | bytes 3145732
  368.2 69.0 %reduce-scatter.14.cloned.1.call-start = ((), (), s32[]{:S(2)}) async-start(), calls=%async_computation.14 | async-start | bytes 163840 | tf_op jit(solution)/shard_map/reduce_scatter | solution.py:230
  411.2 76.5 %reduce-scatter.10.cloned.1.call-start = ((), (), s32[]{:S(2)}) async-start(), calls=%async_computation.12 | async-start | bytes 7864320 | tf_op jit(solution)/shard_map/reduce_scatter | solution.py:229
  419.1 91.3 %reduce-scatter.8.cloned.1.call-start = ((), (), s32[]{:S(2)}) async-start(), calls=%async_computation.10 | async-start | bytes 163840 | tf_op jit(solution)/shard_map/reduce_scatter | solution.py:185
  424.9 159.3 %all-reduce.20.cloned.1.call-start = ((), (), s32[]{:S(2)}) async-start(), calls=%async_computation.15 | async-start | bytes 393216 | tf_op jit(solution)/shard_map/psum | solution.py:258
  429.0 215.4 %reduce-scatter.6.cloned.1.call-start = ((), (), s32[]{:S(2)}) async-start(), calls=%async_computation.9 | async-start | bytes 7864320 | tf_op jit(solution)/shard_map/reduce_scatter | solution.py:179
  434.2 53.5 %copy-start.6 = (bf16[8,1,1,64,768]{4,3,2,1,0:T(8,128)(2,1)S(1)}, bf16[8,1,1,64,768]{4,3,2,1,0:T(8,128)(2,1)}, u32[]{:S(2)}) copy-start(bf16[8,1,1,64,768]{4,3,2,1,0:T(8,128)(2,1)} %copy-done.5) | copy-start | bytes 2359300
  434.2 53.5 %copy-start.67 = (f32[768]{0:T(1024)S(1)}, f32[768]{0:T(1024)}, u32[]{:S(2)}) copy-start(f32[768]{0:T(1024)} %copy-done.66) | copy-start | bytes 9220
  437.2 52.6 %copy-start.29 = (bf16[1,512,768]{2,1,0:T(8,128)(2,1)S(1)}, bf16[1,512,768]{2,1,0:T(8,128)(2,1)}, u32[]{:S(2)}) copy-start(bf16[1,512,768]{2,1,0:T(8,128)(2,1)} %param.25) | copy-start | bytes 2359300
  492.8 17.7 %copy-start.20 = (bf16[512,768]{1,0:T(8,128)(2,1)S(1)}, bf16[512,768]{1,0:T(8,128)(2,1)}, u32[]{:S(2)}) copy-start(bf16[512,768]{1,0:T(8,128)(2,1)} %fusion.62) | copy-start | bytes 2359300
  493.3 19.0 %copy-start.22 = (bf16[512,768]{1,0:T(8,128)(2,1)S(1)}, bf16[512,768]{1,0:T(8,128)(2,1)}, u32[]{:S(2)}) copy-start(bf16[512,768]{1,0:T(8,128)(2,1)} %fusion.67) | copy-start | bytes 2359300
  493.3 19.0 %copy-start.58 = (f32[512,16]{0,1:T(8,128)S(1)}, f32[512,16]{0,1:T(8,128)}, u32[]{:S(2)}) copy-start(f32[512,16]{0,1:T(8,128)} %reduce-scatter.14.cloned.1.call-done) | copy-start | bytes 98308
  500.8 12.6 %copy-start.96 = (s32[8]{0:T(128)S(1)}, s32[8]{0:T(128)}, u32[]{:S(2)}) copy-start(s32[8]{0:T(128)} %get-tuple-element.106) | copy-start | bytes 100
  500.8 12.6 %copy-start.100 = (s32[8]{0:T(128)S(1)}, s32[8]{0:T(128)}, u32[]{:S(2)}) copy-start(s32[8]{0:T(128)} %param.27) | copy-start | bytes 100
  500.8 143.6 %copy-start.54 = (bf16[1,16,768]{2,0,1:T(2,128)(2,1)S(1)}, bf16[1,16,768]{2,0,1:T(2,128)(2,1)}, u32[]{:S(2)}) copy-start(bf16[1,16,768]{2,0,1:T(2,128)(2,1)} %copy-done.53) | copy-start | bytes 73732
  500.8 143.6 %copy-start.78 = (f32[512]{0:T(512)S(1)}, f32[512]{0:T(512)}, u32[]{:S(2)}) copy-start(f32[512]{0:T(512)} %copy-done.77) | copy-start | bytes 6148
  500.9 146.3 %all-to-all-start.1 = ((bf16[8,2,24576]{2,1,0:T(2,128)(2,1)}), bf16[8,2,24576]{2,1,0:T(2,128)(2,1)S(1)}, u32[]{:S(2)}, u32[]{:S(2)}) async-start(bf16[8,2,24576]{2,1,0:T(2,128)(2,1)} %reshape.379), calls=%async_computation.6 | async-start | bytes 1572864 | tf_op jit(solution)/shard_map/all_to_all | solution.py:248
  506.5 277.0 %all-reduce.22.cloned.1.call-start = ((), (), s32[]{:S(2)}) async-start(), calls=%async_computation.16 | async-start | bytes 3145728 | tf_op jit(solution)/shard_map/psum | solution.py:250
  510.4 134.0 %copy-start.59 = (f32[512,16]{0,1:T(8,128)S(1)}, f32[512,16]{0,1:T(8,128)}, u32[]{:S(2)}) copy-start(f32[512,16]{0,1:T(8,128)} %reduce-scatter.8.cloned.1.call-done) | copy-start | bytes 98308
  648.1 141.1 %copy-start.1 = (bf16[8,1,64,768]{3,2,1,0:T(8,128)(2,1)S(1)}, bf16[8,1,64,768]{3,2,1,0:T(8,128)(2,1)}, u32[]{:S(2)}) copy-start(bf16[8,1,64,768]{3,2,1,0:T(8,128)(2,1)} %param.24) | copy-start | bytes 2359300
  (66 other events, 231.0 us)
Sparse Core Ops, SparseCore 0:
  10.8 49.8 all-gather.6
  62.8 27.9 all-gather.8
  93.0 28.5 all-gather.4
  368.3 27.7 reduce-scatter.11
  411.3 15.5 reduce-scatter.13
  429.3 58.3 reduce-scatter.9
  490.8 19.5 reduce-scatter.7
  513.7 70.4 all-reduce.19
  587.0 57.4 reduce-scatter.5
  650.5 132.9 all-reduce.21
